TPU v7x, 128 devices: a whole 4x4x4 slice. The times are simulated.
128 devices in a mesh: dom: 32 (over z, y_lo, x), feat: 4 (over y_hi, core).
Axes of the slice: x: 4, y: 4 (y_hi: 2, y_lo: 2; y = y_hi * 2 + y_lo), z: 4, core: 2. Of those that a mesh axis runs over, the one named last changes fastest.
Arguments:
- items: bfloat16 [8192, 1024], P('dom', 'feat'), may hold values from -6 to 6
- self_ids: int32 [8192], P('dom'), may hold values from 0 to 8191
- neighbor_ids: int32 [8192, 50], P('dom'), may hold values from 0 to 8191
- visit_counts: int32 [8192, 50], P('dom'), may hold values from 1 to 63
- w_self: bfloat16 [1024, 1024], P('feat'), may hold values from -0.1875 to 0.1875
- w_neighbor: bfloat16 [1024, 1024], P('feat'), may hold values from -0.75 to 0.75
- bias: float32 [1024], replicated, may hold values from -3 to 3
Outputs:
- embedding: float32 [8192, 1024], P('dom', 'feat')
All inputs are finite; a program needn't handle non-finite values.
Results may differ from a plain program's by a relative error of at most 0.0018.
Values may be sent and summed in bfloat16 or wider, within the bound.
No kernel may reach another device: no remote copies, remote signals or barrier semaphores. Data moves between devices by JAX's collectives and lax.ppermute only.
A program may use at most 64 MiB of HBM per device.

v0:
```python
import jax
import jax.numpy as jnp
from jax import lax
from jax.sharding import Mesh
from jax.sharding import PartitionSpec as P

DOM = ("dom_0", "dom_1", "dom_2")


def joined_along(tiles, dim):
    lengths = list(tiles.shape[1:])
    lengths[dim] *= tiles.shape[0]
    return jnp.moveaxis(tiles, 0, dim).reshape(lengths)


def stacked_from(value, axes, sequence):
    tiles = value[None]
    for k in sequence:
        tiles = lax.all_gather(tiles, axes[k], axis=0, tiled=True)
    block = [lax.axis_size(axes[k]) for k in reversed(sequence)]
    tiles = tiles.reshape(*block, *value.shape)
    turned = sorted(range(len(sequence)), key=lambda place: sequence[len(sequence) - 1 - place])
    return tiles.transpose(*turned, *range(len(sequence), tiles.ndim)).reshape(-1, *value.shape)


def gathered_by_axis(value, axes, sequence, dim):
    return joined_along(stacked_from(value, axes, sequence), dim)


def in_blocks(value, dim, length):
    before, after = (value.shape[:dim], value.shape[dim + 1 :])
    return jnp.moveaxis(value.reshape(*before, length, -1, *after), dim, 0)


def sent_and_summed(value, axis, dim):
    length = lax.axis_size(axis)
    tiles = lax.all_to_all(in_blocks(value, dim, length), axis, 0, 0, tiled=True)
    return jnp.sum(tiles, axis=0)


def copy_for_each(value, axis):
    length = lax.axis_size(axis)
    return lax.all_to_all(
        jnp.broadcast_to(value[None], (length, *value.shape)), axis, 0, 0, tiled=True
    )


def of_everyone(value, axis):
    everything = copy_for_each(value, axis)
    return jnp.sum(everything, axis=0)


def count_block(target_ids, target_weights, width):
    columns = jnp.arange(width, dtype=jnp.int32)
    match = target_ids[:, :, None] == columns[None, None, :]
    block = jnp.sum(jnp.where(match, target_weights[:, :, None], 0.0), axis=1)
    return block.astype(jnp.bfloat16)


def shards(items, self_ids, neighbor_ids, visit_counts, w_self, w_neighbor, bias):
    batch_rows = self_ids.shape[0]
    counts_float = visit_counts.astype(jnp.float32)
    self_column = self_ids[:, None]
    self_weight = jnp.ones((batch_rows, 1), jnp.float32)
    piece = gathered_by_axis(items, DOM, (1, 0, 2), 0)
    own_block = count_block(self_column, self_weight, piece.shape[0])
    nbr_block = count_block(neighbor_ids, counts_float, piece.shape[0])
    weights = jnp.concatenate([own_block, nbr_block], axis=0)
    sums = jnp.dot(weights, piece, preferred_element_type=jnp.float32)
    own = sums[:batch_rows].astype(jnp.bfloat16)
    nbr_sum = sums[batch_rows:]
    total = jnp.sum(counts_float, axis=1)
    pooled = (nbr_sum / total[:, None]).astype(jnp.bfloat16)
    partial_pre = jnp.dot(own, w_self, preferred_element_type=jnp.float32) + jnp.dot(
        pooled, w_neighbor, preferred_element_type=jnp.float32
    )
    out_share = bias.shape[0] // lax.axis_size("feat")
    column_first = lax.axis_index("feat") * out_share
    pre = sent_and_summed(partial_pre, "feat", 1)
    my_bias = lax.dynamic_slice_in_dim(bias, column_first, out_share, 0)
    hidden = jnp.maximum(pre + my_bias[None, :], 0.0)
    squares = of_everyone(jnp.sum(hidden * hidden, axis=1, keepdims=True), "feat")
    scale = jnp.sqrt(squares / bias.shape[0] + 1e-06)
    return hidden / scale


def solution(mesh):
    torus = Mesh(
        mesh.devices.reshape(4, 2, 4, mesh.shape["feat"]), ("dom_0", "dom_1", "dom_2", "feat")
    )
    placed = (
        P(DOM, "feat"),
        P(DOM),
        P(DOM, None),
        P(DOM, None),
        P("feat", None),
        P("feat", None),
        P(),
    )
    return jax.shard_map(
        shards, mesh=torus, in_specs=placed, out_specs=P(DOM, "feat"), check_vma=False
    )
```

profile of v0, /device:TPU:1, one launch (start us, length us, event | category | flops | bytes accessed | tf_op | source)
XLA Modules:
  0.0 195.1 jit_solution(11336127264499368638)
XLA Ops:
  6.5 0.0 copy-start
  6.5 0.0 copy-start.4
  6.5 0.0 all-gather.4.cloned.1.call-start
  6.5 7.9 %all-gather = bf16[512,256]{1,0:T(8,128)(2,1)} all-gather(bf16[256,256]{1,0:T(8,128)(2,1)} %param.7), channel_id=2, replica_groups=mesh['dom_0'=4,'dom_1'=2,'dom_2'=4,'feat'=4] {'dom_1'}, dimensions={0}, use_global_device_ids=true | all-gather | bytes 393216 | tf_op jit(solution)/shard_map/all_gather | solution.py:19
  14.5 0.0 all-gather.4.cloned.1.call-update
  14.5 0.0 all-gather.6.cloned.1.call-start
  14.6 0.8 convert_element_type.14
  15.4 0.8 convert_reduce_fusion
  16.2 3.7 %select_convert_fusion = bf16[256,8192]{1,0:T(8,128)(2,1)} fusion(s32[256]{0:T(256)} %param.8), kind=kLoop, calls=%fused_computation.6 | loop fusion | flops 6291456 | bytes 4195328 | tf_op jit(solution)/shard_map/convert_element_type | solution.py:57
  20.0 19.6 %all-gather.4.cloned.1.call-done = bf16[8,256,256]{2,1,0:T(8,128)(2,1)} async-done(((bf16[2,256,256]{2,1,0:T(8,128)(2,1)}), bf16[8,256,256]{2,1,0:T(8,128)(2,1)}) %all-gather.4.cloned.1.call-update) | async-done | bytes 1048592 | tf_op jit(solution)/shard_map/all_gather | solution.py:19
  39.6 0.0 all-gather.6.cloned.1.call-update
  39.6 0.0 copy-done.4
  39.6 108.8 %select_reduce_fusion = bf16[256,8192]{1,0:T(8,128)(2,1)} fusion(f32[256,50]{0,1:T(8,128)S(1)} %convert_element_type.14, s32[256,50]{0,1:T(8,128)S(1)} %copy-done.4), kind=kLoop, calls=%fused_computation | loop fusion | flops 312475648 | bytes 4296704 | tf_op jit(solution)/shard_map/reduce_sum | solution.py:56
  148.4 0.0 all-gather.6.cloned.1.call-done
  148.4 0.0 copy-start.1
  148.4 0.0 copy-start.2
  148.5 2.8 %copy.19 = bf16[4,2,4,256,256]{4,3,2,1,0:T(8,128)(2,1)S(1)} copy(bf16[4,2,4,256,256]{4,3,1,0,2:T(8,128)(2,1)} %bitcast.15) | data formatting | bytes 8388608 | tf_op jit(solution)/shard_map/transpose | solution.py:23
  151.2 0.7 copy-done.1
  151.9 1.3 copy-done.2
  153.2 0.0 copy-start.3
  153.2 2.3 %fusion = f32[512,256]{1,0:T(8,128)S(1)} fusion(bf16[8192,256]{1,0:T(8,128)(2,1)S(1)} %bitcast.16, bf16[256,8192]{1,0:T(8,128)(2,1)S(1)} %copy-done.2, bf16[256,8192]{1,0:T(8,128)(2,1)S(1)} %copy-done.1), kind=kOutput, calls=%fused_computation.2 | convolution fusion | flops 2164260864 | bytes 13107200 | tf_op jit(solution)/shard_map/dot_general | solution.py:69
  155.5 0.0 copy-done
  155.5 0.3 fusion.6
  155.8 0.0 copy-done.3
  155.9 0.3 convolution_add_fusion
  156.2 1.1 copy.23
  157.3 7.0 %all-to-all-start = ((f32[4,256,256]{2,1,0:T(8,128)}), f32[4,256,256]{2,1,0:T(8,128)S(1)}, u32[]{:S(2)}, u32[]{:S(2)}) async-start(f32[4,256,256]{2,1,0:T(8,128)} %bitcast.14), calls=%async_computation | async-start | bytes 2097152 | tf_op jit(solution)/shard_map/all_to_all | solution.py:37
  164.3 0.8 dynamic_slice.3
  165.1 14.2 %all-to-all-done = f32[4,256,256]{2,1,0:T(8,128)S(1)} async-done(((f32[4,256,256]{2,1,0:T(8,128)}), f32[4,256,256]{2,1,0:T(8,128)S(1)}, u32[]{:S(2)}, u32[]{:S(2)}) %all-to-all-start) | async-done | bytes 1048608 | tf_op jit(solution)/shard_map/all_to_all | solution.py:37
  179.3 0.1 reduce_sum.51
  179.4 0.1 multiply_reduce_fusion
  179.5 7.9 %all_to_all.10 = f32[4,256,1]{1,2,0:T(1,128)S(1)} all-to-all(f32[4,256,1]{1,2,0:T(1,128)S(1)} %broadcast_in_dim.43), channel_id=1, replica_groups=mesh['dom_0'=4,'dom_1'=2,'dom_2'=4,'feat'=4] {'feat'}, dimensions={0} | all-to-all | bytes 8192 | tf_op jit(solution)/shard_map/all_to_all | solution.py:43
  187.4 0.8 fusion.5
  (3 shorter events, 0.0 us)
Async XLA Ops:
  6.5 149.0 %copy-start = (bf16[256,1024]{1,0:T(8,128)(2,1)S(1)}, bf16[256,1024]{1,0:T(8,128)(2,1)}, u32[]{:S(2)}) copy-start(bf16[256,1024]{1,0:T(8,128)(2,1)} %param.11) | copy-start | bytes 1572868
  6.5 33.1 %copy-start.4 = (s32[256,50]{0,1:T(8,128)S(1)}, s32[256,50]{0,1:T(8,128)}, u32[]{:S(2)}) copy-start(s32[256,50]{0,1:T(8,128)} %param.9) | copy-start | bytes 153604
  6.5 33.0 %all-gather.4.cloned.1.call-start = ((), (), s32[]{:S(2)}) async-start(), calls=%async_computation.2 | async-start | bytes 1310720 | tf_op jit(solution)/shard_map/all_gather | solution.py:19
  14.5 133.9 %all-gather.6.cloned.1.call-start = ((), (), s32[]{:S(2)}) async-start(), calls=%async_computation.3 | async-start | bytes 5242880 | tf_op jit(solution)/shard_map/all_gather | solution.py:19
  148.4 3.4 %copy-start.1 = (bf16[256,8192]{1,0:T(8,128)(2,1)S(1)}, bf16[256,8192]{1,0:T(8,128)(2,1)}, u32[]{:S(2)}) copy-start(bf16[256,8192]{1,0:T(8,128)(2,1)} %select_convert_fusion) | copy-start | bytes 12582916
  148.4 4.7 %copy-start.2 = (bf16[256,8192]{1,0:T(8,128)(2,1)S(1)}, bf16[256,8192]{1,0:T(8,128)(2,1)}, u32[]{:S(2)}) copy-start(bf16[256,8192]{1,0:T(8,128)(2,1)} %select_reduce_fusion) | copy-start | bytes 12582916
  153.2 2.7 %copy-start.3 = (bf16[256,1024]{1,0:T(8,128)(2,1)S(1)}, bf16[256,1024]{1,0:T(8,128)(2,1)}, u32[]{:S(2)}) copy-start(bf16[256,1024]{1,0:T(8,128)(2,1)} %param.12) | copy-start | bytes 1572868
  157.3 22.0 %all-to-all-start = ((f32[4,256,256]{2,1,0:T(8,128)}), f32[4,256,256]{2,1,0:T(8,128)S(1)}, u32[]{:S(2)}, u32[]{:S(2)}) async-start(f32[4,256,256]{2,1,0:T(8,128)} %bitcast.14), calls=%async_computation | async-start | bytes 2097152 | tf_op jit(solution)/shard_map/all_to_all | solution.py:37
Sparse Core Ops, SparseCore 0:
  14.6 24.8 all-gather.3
  41.2 50.2 all-gather.5
where the time goes:
time: 195 us
  other arithmetic  115 us (59%)
  waiting for transfers between devices  33.9 us (17%)
  blocking collectives  15.8 us (8%)
  between operations  13.5 us (7%)
  starting transfers between devices  7.07 us (4%)
  local copies, waits for them, and re-layouts  6.58 us (3%)
  matrix products  2.99 us (2%)
    reduce_sum x1, other arithmetic, count_block(): block = jnp.sum(jnp.where(match, target_weights[:, :, None], 0.0), axis=1)  109 us
    all_gather x2, waiting for transfers between devices, stacked_from(): tiles = lax.all_gather(tiles, axes[k], axis=0, tiled=True)  19.6 us
    all_to_all x1, waiting for transfers between devices, sent_and_summed(): lax.all_to_all(in_blocks(value, dim, length), axis, 0, 0, tiled=True)  14.2 us
    all_gather x1, blocking collectives, stacked_from(): tiles = lax.all_gather(tiles, axes[k], axis=0, tiled=True)  7.94 us
    all_to_all x1, blocking collectives, copy_for_each(): lax.all_to_all(jnp.broadcast_to(value[None], (length, *value.shape)), axi...  7.91 us
    all_to_all x1, starting transfers between devices, sent_and_summed(): lax.all_to_all(in_blocks(value, dim, length), axis, 0, 0, tiled=True)  7.03 us
  transfers between devices with their start and end apart: 3, of which 2 were waited for; matrix products, arithmetic and copies ran while one was open for 59% of the time, Pallas kernels for 0%

commit v1 on v0

--- a/solution.py
+++ b/solution.py
@@ -5,6 +5,11 @@
 from jax.sharding import PartitionSpec as P
 
 DOM = ("dom_0", "dom_1", "dom_2")
+
+
+def swapped_in(x, axis, dim):
+    sent = jnp.stack([x] * lax.axis_size(axis))
+    return jnp.concatenate(lax.all_to_all(sent, axis, 0, 0), axis=dim)
 
 
 def joined_along(tiles, dim):
@@ -16,7 +21,7 @@
 def stacked_from(value, axes, sequence):
     tiles = value[None]
     for k in sequence:
-        tiles = lax.all_gather(tiles, axes[k], axis=0, tiled=True)
+        tiles = swapped_in(tiles, axes[k], 0)
     block = [lax.axis_size(axes[k]) for k in reversed(sequence)]
     tiles = tiles.reshape(*block, *value.shape)
     turned = sorted(range(len(sequence)), key=lambda place: sequence[len(sequence) - 1 - place])

time: 195 us -> 188 us (0.964)
  between operations: 13.5 us -> 0.11 us
  starting transfers between devices: 7.07 us -> 18 us
  waiting for transfers between devices: 33.9 us -> 27.3 us
  local copies, waits for them, and re-layouts: 6.58 us -> 10.1 us
    all_gather x2 -> x0, waiting for transfers between devices: 19.6 us -> none  [stacked_from(): tiles = lax.all_gather(tiles, axes[k], axis=0, tiled=True)]
    all_to_all x0 -> x2, waiting for transfers between devices: none -> 13.1 us  [swapped_in(): return jnp.concatenate(lax.all_to_all(sent, axis, 0, 0), axis=dim)]
    all_to_all x0 -> x2, starting transfers between devices: none -> 10.3 us  [swapped_in(): return jnp.concatenate(lax.all_to_all(sent, axis, 0, 0), axis=dim)]
    all_gather x1 -> x0, blocking collectives: 7.94 us -> none  [stacked_from(): tiles = lax.all_gather(tiles, axes[k], axis=0, tiled=True)]
    all_to_all x0 -> x1, blocking collectives: none -> 7.21 us  [swapped_in(): return jnp.concatenate(lax.all_to_all(sent, axis, 0, 0), axis=dim)]
    another operation x0 -> x2, local copies, waits for them, and re-layouts: none -> 3.51 us  [swapped_in(): sent = jnp.stack([x] * lax.axis_size(axis))]
    all_to_all x0 -> x1, local copies, waits for them, and re-layouts: none -> 2.76 us  [swapped_in(): return jnp.concatenate(lax.all_to_all(sent, axis, 0, 0), axis=dim)]
    transpose x1 -> x0, local copies, waits for them, and re-layouts: 2.76 us -> none  [stacked_from(): tiles.transpose(*turned, *range(len(sequence), tiles.ndim))]
  transfers between devices with their start and end apart: 3 -> 3, of which waited for: 2 -> 2; matrix products, arithmetic and copies ran while one was open for 59% -> 60% of each run, Pallas kernels for 0% -> 0%
where the time goes in v1:
time: 188 us
  other arithmetic  114 us (61%)
  waiting for transfers between devices  27.3 us (15%)
  starting transfers between devices  18 us (10%)
  blocking collectives  15.1 us (8%)
  local copies, waits for them, and re-layouts  10.1 us (5%)
  matrix products  2.98 us (2%)
    reduce_sum x1, other arithmetic, count_block(): block = jnp.sum(jnp.where(match, target_weights[:, :, None], 0.0), axis=1)  109 us
    all_to_all x1, waiting for transfers between devices, sent_and_summed(): lax.all_to_all(in_blocks(value, dim, length), axis, 0, 0, tiled=True)  14.2 us
    all_to_all x2, waiting for transfers between devices, swapped_in(): return jnp.concatenate(lax.all_to_all(sent, axis, 0, 0), axis=dim)  13.1 us
    all_to_all x2, starting transfers between devices, swapped_in(): return jnp.concatenate(lax.all_to_all(sent, axis, 0, 0), axis=dim)  10.3 us
    all_to_all x1, blocking collectives, copy_for_each(): lax.all_to_all(jnp.broadcast_to(value[None], (length, *value.shape)), axi...  7.91 us
    all_to_all x1, starting transfers between devices, sent_and_summed(): lax.all_to_all(in_blocks(value, dim, length), axis, 0, 0, tiled=True)  7.65 us
    all_to_all x1, blocking collectives, swapped_in(): return jnp.concatenate(lax.all_to_all(sent, axis, 0, 0), axis=dim)  7.21 us
  transfers between devices with their start and end apart: 3, of which 2 were waited for; matrix products, arithmetic and copies ran while one was open for 60% of the time, Pallas kernels for 0%

profile of v1, /device:TPU:1, one launch (start us, length us, event | category | flops | bytes accessed | tf_op | source)
XLA Modules:
  0.0 187.6 jit_solution(8486941571046100140)
XLA Ops:
  0.0 0.0 copy-start
  0.0 0.0 copy-start.4
  0.0 1.1 pad_maximum_fusion
  1.1 7.2 %all_to_all.25 = bf16[2,1,256,256]{3,2,1,0:T(8,128)(2,1)S(1)} all-to-all(bf16[2,1,256,256]{3,2,1,0:T(8,128)(2,1)S(1)} %pad_maximum_fusion), channel_id=1, replica_groups=mesh['dom_0'=4,'dom_1'=2,'dom_2'=4,'feat'=4] {'dom_1'}, dimensions={0} | all-to-all | bytes 524288 | tf_op jit(solution)/shard_map/all_to_all | solution.py:12
  8.3 1.1 stack.10
  9.3 5.4 %all-to-all-start.1 = ((bf16[4,2,256,256]{3,2,1,0:T(8,128)(2,1)}), bf16[4,2,256,256]{3,2,1,0:T(8,128)(2,1)S(1)}, u32[]{:S(2)}, u32[]{:S(2)}) async-start(bf16[4,2,256,256]{3,2,1,0:T(8,128)(2,1)} %stack.10), calls=%async_computation.1 | async-start | bytes 2097152 | tf_op jit(solution)/shard_map/all_to_all | solution.py:12
  14.7 0.0 copy-done.4
  14.7 13.1 %all-to-all-done.1 = bf16[4,2,256,256]{3,2,1,0:T(8,128)(2,1)S(1)} async-done(((bf16[4,2,256,256]{3,2,1,0:T(8,128)(2,1)}), bf16[4,2,256,256]{3,2,1,0:T(8,128)(2,1)S(1)}, u32[]{:S(2)}, u32[]{:S(2)}) %all-to-all-start.1) | async-done | bytes 1048608 | tf_op jit(solution)/shard_map/all_to_all | solution.py:12
  27.8 2.5 %stack.11 = bf16[4,8,256,256]{3,2,1,0:T(8,128)(2,1)} broadcast(bf16[8,256,256]{2,1,0:T(8,128)(2,1)S(1)} %bitcast.18), dimensions={1,2,3} | broadcast | bytes 5242880 | tf_op jit(solution)/shard_map/stack | solution.py:11
  30.3 0.0 copy-start.5
  30.3 5.0 %all-to-all-start.2 = ((bf16[4,8,256,256]{3,2,1,0:T(8,128)(2,1)}), bf16[4,8,256,256]{3,2,1,0:T(8,128)(2,1)}, u32[]{:S(2)}, u32[]{:S(2)}) async-start(bf16[4,8,256,256]{3,2,1,0:T(8,128)(2,1)} %stack.11), calls=%async_computation.2 | async-start | bytes 8388608 | tf_op jit(solution)/shard_map/all_to_all | solution.py:12
  35.3 0.0 copy-done.5
  35.3 0.0 copy-start.6
  35.3 108.8 %select_reduce_fusion = bf16[256,8192]{1,0:T(8,128)(2,1)} fusion(f32[256,50]{0,1:T(8,128)S(1)} %convert_element_type.14, s32[256,50]{0,1:T(8,128)S(1)} %copy-done.5), kind=kLoop, calls=%fused_computation | loop fusion | flops 312475648 | bytes 4296704 | tf_op jit(solution)/shard_map/reduce_sum | solution.py:61
  144.1 0.0 copy-done.6
  144.1 3.1 %select_convert_fusion = bf16[256,8192]{1,0:T(8,128)(2,1)} fusion(s32[256]{0:T(256)S(1)} %copy-done.6), kind=kLoop, calls=%fused_computation.6 | loop fusion | flops 6291456 | bytes 4195328 | tf_op jit(solution)/shard_map/convert_element_type | solution.py:62
  147.2 0.0 all-to-all-done.2
  147.2 0.0 copy-start.1
  147.2 0.0 copy-start.2
  147.2 2.8 %copy.16 = bf16[4,8,256,256]{3,2,0,1:T(8,128)(2,1)S(1)} copy(bf16[4,8,256,256]{3,2,1,0:T(8,128)(2,1)} %all-to-all-done.2) | data formatting | bytes 8388608 | tf_op jit(solution)/shard_map/all_to_all | solution.py:12
  150.0 0.7 copy-done.1
  150.6 1.3 copy-done.2
  151.9 0.0 copy-start.3
  151.9 2.3 %fusion = f32[512,256]{1,0:T(8,128)S(1)} fusion(bf16[8192,256]{1,0:T(8,128)(2,1)S(1)} %bitcast.19, bf16[256,8192]{1,0:T(8,128)(2,1)S(1)} %copy-done.2, bf16[256,8192]{1,0:T(8,128)(2,1)S(1)} %copy-done.1), kind=kOutput, calls=%fused_computation.2 | convolution fusion | flops 2164260864 | bytes 13107200 | tf_op jit(solution)/shard_map/dot_general | solution.py:74
  154.3 0.0 copy-done
  154.3 0.3 fusion.6
  154.6 0.0 copy-done.3
  154.6 0.3 convolution_add_fusion
  154.9 1.1 copy.20
  156.0 7.7 %all-to-all-start.3 = ((f32[4,256,256]{2,1,0:T(8,128)}), f32[4,256,256]{2,1,0:T(8,128)S(1)}, u32[]{:S(2)}, u32[]{:S(2)}) async-start(f32[4,256,256]{2,1,0:T(8,128)} %bitcast.17), calls=%async_computation.3 | async-start | bytes 2097152 | tf_op jit(solution)/shard_map/all_to_all | solution.py:42
  163.7 0.8 dynamic_slice.3
  164.4 14.2 %all-to-all-done.3 = f32[4,256,256]{2,1,0:T(8,128)S(1)} async-done(((f32[4,256,256]{2,1,0:T(8,128)}), f32[4,256,256]{2,1,0:T(8,128)S(1)}, u32[]{:S(2)}, u32[]{:S(2)}) %all-to-all-start.3) | async-done | bytes 1048608 | tf_op jit(solution)/shard_map/all_to_all | solution.py:42
  178.7 0.1 reduce_sum.51
  178.7 0.1 multiply_reduce_fusion
  178.9 7.9 %all_to_all.26 = f32[4,256,1]{1,2,0:T(1,128)S(1)} all-to-all(f32[4,256,1]{1,2,0:T(1,128)S(1)} %broadcast_in_dim.39), channel_id=1, replica_groups=mesh['dom_0'=4,'dom_1'=2,'dom_2'=4,'feat'=4] {'feat'}, dimensions={0} | all-to-all | bytes 8192 | tf_op jit(solution)/shard_map/all_to_all | solution.py:48
  186.8 0.8 fusion.5
  (5 shorter events, 0.1 us)
Async XLA Ops:
  0.0 154.3 %copy-start = (bf16[256,1024]{1,0:T(8,128)(2,1)S(1)}, bf16[256,1024]{1,0:T(8,128)(2,1)}, u32[]{:S(2)}) copy-start(bf16[256,1024]{1,0:T(8,128)(2,1)} %param.11) | copy-start | bytes 1572868
  0.0 14.7 %copy-start.4 = (s32[256,50]{0,1:T(8,128)S(1)}, s32[256,50]{0,1:T(8,128)}, u32[]{:S(2)}) copy-start(s32[256,50]{0,1:T(8,128)} %param.10) | copy-start | bytes 153604
  9.3 18.5 %all-to-all-start.1 = ((bf16[4,2,256,256]{3,2,1,0:T(8,128)(2,1)}), bf16[4,2,256,256]{3,2,1,0:T(8,128)(2,1)S(1)}, u32[]{:S(2)}, u32[]{:S(2)}) async-start(bf16[4,2,256,256]{3,2,1,0:T(8,128)(2,1)} %stack.10), calls=%async_computation.1 | async-start | bytes 2097152 | tf_op jit(solution)/shard_map/all_to_all | solution.py:12
  30.3 5.0 %copy-start.5 = (s32[256,50]{0,1:T(8,128)S(1)}, s32[256,50]{0,1:T(8,128)}, u32[]{:S(2)}) copy-start(s32[256,50]{0,1:T(8,128)} %param.9) | copy-start | bytes 153604
  30.3 116.9 %all-to-all-start.2 = ((bf16[4,8,256,256]{3,2,1,0:T(8,128)(2,1)}), bf16[4,8,256,256]{3,2,1,0:T(8,128)(2,1)}, u32[]{:S(2)}, u32[]{:S(2)}) async-start(bf16[4,8,256,256]{3,2,1,0:T(8,128)(2,1)} %stack.11), calls=%async_computation.2 | async-start | bytes 8388608 | tf_op jit(solution)/shard_map/all_to_all | solution.py:12
  35.3 108.8 %copy-start.6 = (s32[256]{0:T(256)S(1)}, s32[256]{0:T(256)}, u32[]{:S(2)}) copy-start(s32[256]{0:T(256)} %param.8) | copy-start | bytes 3076
  147.2 3.5 %copy-start.1 = (bf16[256,8192]{1,0:T(8,128)(2,1)S(1)}, bf16[256,8192]{1,0:T(8,128)(2,1)}, u32[]{:S(2)}) copy-start(bf16[256,8192]{1,0:T(8,128)(2,1)} %select_convert_fusion) | copy-start | bytes 12582916
  147.2 4.7 %copy-start.2 = (bf16[256,8192]{1,0:T(8,128)(2,1)S(1)}, bf16[256,8192]{1,0:T(8,128)(2,1)}, u32[]{:S(2)}) copy-start(bf16[256,8192]{1,0:T(8,128)(2,1)} %select_reduce_fusion) | copy-start | bytes 12582916
  151.9 2.7 %copy-start.3 = (bf16[256,1024]{1,0:T(8,128)(2,1)S(1)}, bf16[256,1024]{1,0:T(8,128)(2,1)}, u32[]{:S(2)}) copy-start(bf16[256,1024]{1,0:T(8,128)(2,1)} %param.12) | copy-start | bytes 1572868
  156.0 22.6 %all-to-all-start.3 = ((f32[4,256,256]{2,1,0:T(8,128)}), f32[4,256,256]{2,1,0:T(8,128)S(1)}, u32[]{:S(2)}, u32[]{:S(2)}) async-start(f32[4,256,256]{2,1,0:T(8,128)} %bitcast.17), calls=%async_computation.3 | async-start | bytes 2097152 | tf_op jit(solution)/shard_map/all_to_all | solution.py:42
